TPU v7x, 256 devices: a whole 4x4x8 slice. The times are simulated.
256 devices in a mesh: seq: 64 (over z, y_hi, x), tp: 4 (over y_lo, core).
Axes of the slice: x: 4, y: 4 (y_hi: 2, y_lo: 2; y = y_hi * 2 + y_lo), z: 8, core: 2. Of those that a mesh axis runs over, the one named last changes fastest.
Arguments:
- queries: bfloat16 [16384, 8192], P('seq', 'tp'), may hold values from -150 to 150
- new_key_value: bfloat16 [2, 16384, 1024], P(None, 'seq', 'tp'), may hold values from -6 to 6
- page_slot: int32 [2048], P('seq'), may hold values from 0 to 2047, as said below
Outputs:
- attended: bfloat16 [16384, 8192], P('seq', 'tp')
- kv_pool: bfloat16 [2, 2048, 8, 1024], P(None, 'seq', None, 'tp')
Inputs may be any that keep to these rules, and one draw needn't show every extreme that they name: `page_slot`: each of the 2048 pool slots is named by exactly one page; slots k * 32 to (k + 1) * 32 - 1 are held by index k of seq. The 32 pages of one sequence block go to 32 different owners, one page to each; for each position j of a page within its block, the j-th pages of all blocks go to different owners.
All inputs are finite; a program needn't handle non-finite values.
Results may differ from a plain program's by a relative error of at most 0.0055.
Values may be sent and summed in bfloat16 or wider, within the bound.
A program may use at most 64 MiB of HBM per device.

v0:
```python
import math

import jax
import jax.numpy as jnp
from jax import lax
from jax.sharding import PartitionSpec as P

QUERY_HEADS = 64
KEY_VALUE_HEADS = 8
HEAD_SIZE = 128
PAGE_TOKENS = 8
STEPS = 7


masked_score = -1e30


def passed_along(value, axis, by):
    devices = lax.axis_size(axis)
    pairs = [(i, i + by) for i in range(devices) if 0 <= i + by < devices]
    return lax.ppermute(value, axis, pairs)


def attend(queries, new_key_value):
    tok_rows = queries.shape[0]
    query_group = QUERY_HEADS // KEY_VALUE_HEADS
    heads_kv = new_key_value.shape[2] // HEAD_SIZE
    query_heads = queries.reshape(tok_rows, heads_kv, query_group, HEAD_SIZE)
    scale = 1.0 / math.sqrt(HEAD_SIZE)
    self_index = lax.axis_index("seq")
    places = jnp.arange(tok_rows)
    causal = places[None, :] <= places[:, None]

    def absorb(state, block, distance):
        top, total, mixed = state
        key_rows = block[0].reshape(tok_rows, heads_kv, HEAD_SIZE)
        value_rows = block[1].reshape(tok_rows, heads_kv, HEAD_SIZE)
        score = (
            jnp.einsum("ikgd,jkd->kgij", query_heads, key_rows, preferred_element_type=jnp.float32)
            * scale
        )
        allowed = causal if distance == 0 else jnp.full(causal.shape, True)
        allowed = jnp.logical_and(allowed, self_index >= distance)
        score = jnp.where(allowed, score, masked_score)
        new_top = jnp.maximum(top, jnp.max(score, -1))
        fade = jnp.exp(top - new_top)
        weight = jnp.where(allowed, jnp.exp(score - new_top[..., None]), 0.0)
        total = total * fade + jnp.sum(weight, -1)
        mixed = mixed * jnp.transpose(fade, (2, 0, 1))[..., None] + jnp.einsum(
            "kgij,jkd->ikgd",
            weight.astype(jnp.bfloat16),
            value_rows,
            preferred_element_type=jnp.float32,
        )
        return (new_top, total, mixed)

    state = (
        jnp.full((heads_kv, query_group, tok_rows), masked_score, jnp.float32),
        jnp.zeros((heads_kv, query_group, tok_rows), jnp.float32),
        jnp.zeros((tok_rows, heads_kv, query_group, HEAD_SIZE), jnp.float32),
    )
    state = absorb(state, new_key_value, 0)
    for distance in range(1, STEPS):
        remote = passed_along(new_key_value, "seq", distance)
        state = absorb(state, remote, distance)
    top, total, mixed = state
    result = mixed / jnp.transpose(total, (2, 0, 1))[..., None]
    return result.astype(jnp.bfloat16).reshape(tok_rows, heads_kv * query_group * HEAD_SIZE)


def place_pages(new_key_value, page_slot):
    pages_dev = page_slot.shape[0]
    width = new_key_value.shape[2]
    page_table = new_key_value.reshape(2, pages_dev, PAGE_TOKENS, width)
    slot_range = jnp.arange(pages_dev)
    owners = lax.axis_size("seq")
    per_owner = (pages_dev + owners - 1) // owners
    owner = page_slot // pages_dev
    within = page_slot % pages_dev
    rank = slot_range % per_owner
    pick = jnp.logical_and(
        owner[None, None, :] == jnp.arange(owners)[:, None, None],
        rank[None, None, :] == jnp.arange(per_owner)[None, :, None],
    )
    outgoing = jnp.einsum(
        "orj,cjtf->cortf", pick.astype(jnp.bfloat16), page_table, preferred_element_type=jnp.float32
    ).astype(jnp.bfloat16)
    label = jnp.sum(jnp.where(pick, within[None, None, :] + 1, 0), axis=2)[None]
    arrived, labels = (
        lax.all_to_all(outgoing, "seq", split_axis=1, concat_axis=1, tiled=True),
        lax.all_to_all(label, "seq", split_axis=1, concat_axis=1, tiled=True),
    )
    place = labels[0][None, :, :] - 1 == slot_range[:, None, None]
    pool = jnp.einsum(
        "wor,cortf->cwtf", place.astype(jnp.bfloat16), arrived, preferred_element_type=jnp.float32
    )
    return pool.astype(jnp.bfloat16)


def body(queries, new_key_value, page_slot):
    attended = attend(queries, new_key_value)
    kv_pool = place_pages(new_key_value, page_slot)
    return (attended, kv_pool)


def solution(mesh):
    placed = (P("seq", "tp"), P(None, "seq", "tp"), P("seq"))
    return jax.shard_map(
        body,
        mesh=mesh,
        in_specs=placed,
        out_specs=(P("seq", "tp"), P(None, "seq", None, "tp")),
        check_vma=False,
    )
```

profile of v0, /device:TPU:32, one launch (start us, length us, event | category | flops | bytes accessed | tf_op | source)
XLA Modules:
  0.0 96.7 jit_solution(17035687276532012948)
XLA Ops:
  0.6 1.1 %copy.131 = bf16[2,256,256]{1,2,0:T(8,128)(2,1)S(1)} copy(bf16[2,256,256]{2,1,0:T(8,128)(2,1)} %param.4) | data formatting | bytes 524288 | tf_op args[1]
  1.8 3.4 %collective-permute-start = (bf16[2,256,256]{1,2,0:T(8,128)(2,1)S(1)}, bf16[2,256,256]{1,2,0:T(8,128)(2,1)}, u32[]{:S(2)}, u32[]{:S(2)}) collective-permute-start(bf16[2,256,256]{1,2,0:T(8,128)(2,1)S(1)} %copy.131), channel_id=1, source_target_pairs={{0,4},{4,8},{8,12},{12,16},{16,20},{20,24},{24,28},{28,32},{32,36}... | collective-permute-start | bytes 786440 | tf_op jit(solution)/shard_map/ppermute | solution.py:21
  5.2 7.3 %collective-permute-start.5 = (bf16[2,256,256]{1,2,0:T(8,128)(2,1)S(1)}, bf16[2,256,256]{1,2,0:T(8,128)(2,1)S(1)}, u32[]{:S(2)}, u32[]{:S(2)}) collective-permute-start(bf16[2,256,256]{1,2,0:T(8,128)(2,1)S(1)} %copy.131), channel_id=1, source_target_pairs={{0,24},{4,28},{8,32},{12,36},{16,40},{20,44},{24,48},{28,52},{32,5... | collective-permute-start | bytes 786440 | tf_op jit(solution)/shard_map/ppermute | solution.py:21
  12.5 5.5 %collective-permute-start.4 = (bf16[2,256,256]{1,2,0:T(8,128)(2,1)S(1)}, bf16[2,256,256]{1,2,0:T(8,128)(2,1)S(1)}, u32[]{:S(2)}, u32[]{:S(2)}) collective-permute-start(bf16[2,256,256]{1,2,0:T(8,128)(2,1)S(1)} %copy.131), channel_id=1, source_target_pairs={{0,20},{4,24},{8,28},{12,32},{16,36},{20,40},{24,44},{28,48},{32,5... | collective-permute-start | bytes 786440 | tf_op jit(solution)/shard_map/ppermute | solution.py:21
  18.0 3.6 %collective-permute-start.3 = (bf16[2,256,256]{1,2,0:T(8,128)(2,1)S(1)}, bf16[2,256,256]{1,2,0:T(8,128)(2,1)S(1)}, u32[]{:S(2)}, u32[]{:S(2)}) collective-permute-start(bf16[2,256,256]{1,2,0:T(8,128)(2,1)S(1)} %copy.131), channel_id=1, source_target_pairs={{0,16},{4,20},{8,24},{12,28},{16,32},{20,36},{24,40},{28,44},{32,4... | collective-permute-start | bytes 786440 | tf_op jit(solution)/shard_map/ppermute | solution.py:21
  21.6 2.9 %collective-permute-start.2 = (bf16[2,256,256]{1,2,0:T(8,128)(2,1)S(1)}, bf16[2,256,256]{1,2,0:T(8,128)(2,1)S(1)}, u32[]{:S(2)}, u32[]{:S(2)}) collective-permute-start(bf16[2,256,256]{1,2,0:T(8,128)(2,1)S(1)} %copy.131), channel_id=1, source_target_pairs={{0,12},{4,16},{8,20},{12,24},{16,28},{20,32},{24,36},{28,40},{32,4... | collective-permute-start | bytes 786440 | tf_op jit(solution)/shard_map/ppermute | solution.py:21
  26.0 10.7 %all-to-all-start.1 = ((s32[1,64,1]{2,0,1:T(1,128)}), s32[1,64,1]{2,0,1:T(1,128)S(1)}, u32[]{:S(2)}, u32[]{:S(2)}) async-start(s32[1,64,1]{2,0,1:T(1,128)} %copy.163), calls=%async_computation.1 | async-start | bytes 65536 | tf_op jit(solution)/shard_map/all_to_all | solution.py:91
  36.7 1.5 %copy.203 = bf16[32,8,16,128]{3,2,1,0:T(8,128)(2,1)S(1)} copy(bf16[32,8,16,128]{3,1,2,0:T(8,128)(2,1)} %bitcast.362) | data formatting | bytes 2097152
  38.2 2.9 %fusion.12 = (f32[2,8,256]{2,1,0:T(8,128)S(1)}, f32[2,256,256,8]{2,1,3,0:T(8,128)}) fusion(pred[256,256]{0,1:T(8,128)(4,1)S(1)} %fusion.111, bf16[256,2,128,1]{0,2,3,1:T(8,128)(2,1)S(1)} %bitcast.364, bf16[256,2,8,128]{3,2,1,0:T(8,128)(2,1)S(1)} %bitcast.354), kind=kOutput, calls=%fused_computation.32 | convolution fusion | flops 271577088 | bytes 5455872 | tf_op jit(solution)/shard_map/ikgd,jkd->kgij/dot_general | solution.py:39
  42.8 4.8 %all-to-all-done.1 = s32[1,64,1]{2,0,1:T(1,128)S(1)} async-done(((s32[1,64,1]{2,0,1:T(1,128)}), s32[1,64,1]{2,0,1:T(1,128)S(1)}, u32[]{:S(2)}, u32[]{:S(2)}) %all-to-all-start.1) | async-done | bytes 288 | tf_op jit(solution)/shard_map/all_to_all | solution.py:91
  47.6 7.9 %all-to-all-start = ((bf16[2,64,1,8,256]{4,3,0,2,1:T(8,128)(2,1)}), bf16[2,64,1,8,256]{4,3,0,2,1:T(8,128)(2,1)S(1)}, u32[]{:S(2)}, u32[]{:S(2)}) async-start(bf16[2,64,1,8,256]{4,3,0,2,1:T(8,128)(2,1)} %copy.161), calls=%async_computation | async-start | bytes 1048576 | tf_op jit(solution)/shard_map/all_to_all | solution.py:90
  55.5 1.2 %add_reduce_fusion = s32[64]{0:T(128)S(1)} fusion(s32[1,64,1]{2,0,1:T(1,128)S(1)} %all-to-all-done.1), kind=kLoop, calls=%fused_computation.133 | loop fusion | flops 64 | bytes 512 | tf_op jit(solution)/shard_map/sub | solution.py:93
  56.7 5.1 %collective-permute-start.1 = (bf16[2,256,256]{1,2,0:T(8,128)(2,1)S(1)}, bf16[2,256,256]{1,2,0:T(8,128)(2,1)S(1)}, u32[]{:S(2)}, u32[]{:S(2)}) collective-permute-start(bf16[2,256,256]{1,2,0:T(8,128)(2,1)S(1)} %copy.131), channel_id=1, source_target_pairs={{0,8},{4,12},{8,16},{12,20},{16,24},{20,28},{24,32},{28,36},{32,40... | collective-permute-start | bytes 786440 | tf_op jit(solution)/shard_map/ppermute | solution.py:21
  67.6 8.3 %collective-permute-done.1 = bf16[2,256,256]{1,2,0:T(8,128)(2,1)S(1)} collective-permute-done((bf16[2,256,256]{1,2,0:T(8,128)(2,1)S(1)}, bf16[2,256,256]{1,2,0:T(8,128)(2,1)S(1)}, u32[]{:S(2)}, u32[]{:S(2)}) %collective-permute-start.1) | collective-permute-done | bytes 262176 | tf_op jit(solution)/shard_map/ppermute | solution.py:21
  79.0 2.2 %fusion.13 = (f32[2,8,256]{2,1,0:T(8,128)S(1)}, f32[2,8,256]{2,1,0:T(8,128)S(1)}) fusion(f32[2,256,256,8]{2,1,3,0:T(8,128)S(1)} %copy-done, f32[2,8,256]{2,1,0:T(8,128)S(1)} %get-tuple-element.39, pred[256,256]{0,1:T(8,128)(4,1)S(1)} %fusion.111, f32[2,8,256]{2,1,0:T(8,128)S(1)} %get-tuple-element.23, f32[2,256,256,8]{2,1,3,0:T(8,128)S(1)} %get-tuple-element.53, ...), kind=kLoop, calls=%fused_computation.33 | loop fusion | flops 10477568 | bytes 8519681 | tf_op jit(solution)/shard_map/reduce_sum | solution.py:48
  81.2 1.2 %fusion.39 = f32[2,8,256,128]{2,3,1,0:T(8,128)S(1)} fusion(bf16[256,2,128,1]{0,2,3,1:T(8,128)(2,1)S(1)} %bitcast.371, f32[2,256,256,8]{2,1,3,0:T(8,128)S(1)} %copy-done, f32[2,8,256]{2,1,0:T(8,128)S(1)} %get-tuple-element.39, pred[256,256]{0,1:T(8,128)(4,1)S(1)} %fusion.111), kind=kOutput, calls=%fused_computation.53 | convolution fusion | flops 273678336 | bytes 6504448 | tf_op jit(solution)/shard_map/kgij,jkd->ikgd/dot_general | solution.py:49
  82.4 1.1 %fusion.35 = f32[2,8,256,128]{2,3,1,0:T(8,128)S(1)} fusion(bf16[256,2,128,1]{0,2,3,1:T(8,128)(2,1)S(1)} %bitcast.377, f32[2,256,256,8]{2,1,3,0:T(8,128)S(1)} %get-tuple-element.51, f32[2,8,256]{2,1,0:T(8,128)S(1)} %get-tuple-element.22, pred[]{:T(512)S(6)} %ge.23), kind=kOutput, calls=%fused_computation.51 | convolution fusion | flops 273678336 | bytes 6438913 | tf_op jit(solution)/shard_map/kgij,jkd->ikgd/dot_general | solution.py:49
  83.5 2.0 %fusion.17 = (f32[2,8,256]{2,1,0:T(8,128)S(1)}, f32[2,8,256]{2,1,0:T(8,128)S(1)}) fusion(f32[2,256,256,8]{2,1,3,0:T(8,128)S(1)} %get-tuple-element.51, f32[2,8,256]{2,1,0:T(8,128)S(1)} %get-tuple-element.22, pred[]{:T(512)S(6)} %ge.23, f32[2,8,256]{2,1,0:T(8,128)S(1)} %get-tuple-element.21, f32[2,256,256,8]{2,1,3,0:T(8,128)S(1)} %get-tuple-element.49, ...), kind=kLoop, calls=%fused_computation.37 | loop fusion | flops 10477568 | bytes 8454146 | tf_op jit(solution)/shard_map/reduce_sum | solution.py:48
  85.6 1.1 %fusion.33 = f32[2,8,256,128]{2,3,1,0:T(8,128)S(1)} fusion(bf16[256,2,128,1]{0,2,3,1:T(8,128)(2,1)S(1)} %bitcast.376, f32[2,256,256,8]{2,1,3,0:T(8,128)S(1)} %get-tuple-element.49, f32[2,8,256]{2,1,0:T(8,128)S(1)} %get-tuple-element.21, pred[]{:T(512)S(6)} %ge.24), kind=kOutput, calls=%fused_computation.50 | convolution fusion | flops 273678336 | bytes 6438913 | tf_op jit(solution)/shard_map/kgij,jkd->ikgd/dot_general | solution.py:49
  86.7 1.1 %fusion.31 = f32[2,8,256,128]{2,3,1,0:T(8,128)S(1)} fusion(bf16[256,2,128,1]{0,2,3,1:T(8,128)(2,1)S(1)} %bitcast.375, f32[2,256,256,8]{2,1,3,0:T(8,128)S(1)} %get-tuple-element.47, f32[2,8,256]{2,1,0:T(8,128)S(1)} %get-tuple-element.20, pred[]{:T(512)S(6)} %ge.25), kind=kOutput, calls=%fused_computation.49 | convolution fusion | flops 273678336 | bytes 6438913 | tf_op jit(solution)/shard_map/kgij,jkd->ikgd/dot_general | solution.py:49
  87.8 2.0 %fusion.21 = (f32[2,8,256]{2,1,0:T(8,128)S(1)}, f32[2,8,256]{2,1,0:T(8,128)S(1)}) fusion(f32[2,256,256,8]{2,1,3,0:T(8,128)S(1)} %get-tuple-element.47, f32[2,8,256]{2,1,0:T(8,128)S(1)} %get-tuple-element.20, pred[]{:T(512)S(6)} %ge.25, f32[2,8,256]{2,1,0:T(8,128)S(1)} %get-tuple-element.19, f32[2,256,256,8]{2,1,3,0:T(8,128)S(1)} %get-tuple-element.45, ...), kind=kLoop, calls=%fused_computation.41 | loop fusion | flops 10477568 | bytes 8454146 | tf_op jit(solution)/shard_map/reduce_sum | solution.py:48
  89.8 1.1 %fusion.29 = f32[2,8,256,128]{2,3,1,0:T(8,128)S(1)} fusion(bf16[256,2,128,1]{0,2,3,1:T(8,128)(2,1)S(1)} %bitcast.373, f32[2,256,256,8]{2,1,3,0:T(8,128)S(1)} %get-tuple-element.45, f32[2,8,256]{2,1,0:T(8,128)S(1)} %get-tuple-element.19, pred[]{:T(512)S(6)} %ge.26), kind=kOutput, calls=%fused_computation.48 | convolution fusion | flops 273678336 | bytes 6438913 | tf_op jit(solution)/shard_map/kgij,jkd->ikgd/dot_general | solution.py:49
  92.0 2.1 %fusion.42 = bf16[256,2,8,128]{0,3,2,1:T(8,128)(2,1)S(1)} fusion(f32[2,8,256,128]{2,3,1,0:T(8,128)S(1)} %fusion.29, f32[2,8,256,128]{2,3,1,0:T(8,128)S(1)} %fusion.31, f32[2,8,256,128]{2,3,1,0:T(8,128)S(1)} %fusion.33, f32[2,8,256,128]{2,3,1,0:T(8,128)S(1)} %fusion.35, f32[2,8,256,128]{2,3,1,0:T(8,128)S(1)} %fusion.37, f32[2,8,256,128]{2,3,1,0:T(8,128)S(1)} %fusion.39, ...), kind=kOutput, calls=%fused_computation.56 | convolution fusion | flops 281542656 | bytes 18104320 | tf_op jit(solution)/shard_map/kgij,jkd->ikgd/dot_general | solution.py:49
  94.1 1.4 %copy.164 = bf16[256,2048]{1,0:T(8,128)(2,1)} copy(bf16[256,2048]{0,1:T(8,128)(2,1)S(1)} %bitcast.363) | data formatting | bytes 2097152
  (38 shorter events, 14.1 us)
Async XLA Ops:
  0.6 40.5 %copy-start.1 = (bf16[2,256,256]{2,1,0:T(8,128)(2,1)S(1)}, bf16[2,256,256]{2,1,0:T(8,128)(2,1)}, u32[]{:S(2)}) copy-start(bf16[2,256,256]{2,1,0:T(8,128)(2,1)} %param.4) | copy-start | bytes 786436
  1.8 54.9 %collective-permute-start = (bf16[2,256,256]{1,2,0:T(8,128)(2,1)S(1)}, bf16[2,256,256]{1,2,0:T(8,128)(2,1)}, u32[]{:S(2)}, u32[]{:S(2)}) collective-permute-start(bf16[2,256,256]{1,2,0:T(8,128)(2,1)S(1)} %copy.131), channel_id=1, source_target_pairs={{0,4},{4,8},{8,12},{12,16},{16,20},{20,24},{24,28},{28,32},{32,36}... | collective-permute-start | bytes 786440 | tf_op jit(solution)/shard_map/ppermute | solution.py:21
  5.2 58.5 %collective-permute-start.5 = (bf16[2,256,256]{1,2,0:T(8,128)(2,1)S(1)}, bf16[2,256,256]{1,2,0:T(8,128)(2,1)S(1)}, u32[]{:S(2)}, u32[]{:S(2)}) collective-permute-start(bf16[2,256,256]{1,2,0:T(8,128)(2,1)S(1)} %copy.131), channel_id=1, source_target_pairs={{0,24},{4,28},{8,32},{12,36},{16,40},{20,44},{24,48},{28,52},{32,5... | collective-permute-start | bytes 786440 | tf_op jit(solution)/shard_map/ppermute | solution.py:21
  12.5 52.2 %collective-permute-start.4 = (bf16[2,256,256]{1,2,0:T(8,128)(2,1)S(1)}, bf16[2,256,256]{1,2,0:T(8,128)(2,1)S(1)}, u32[]{:S(2)}, u32[]{:S(2)}) collective-permute-start(bf16[2,256,256]{1,2,0:T(8,128)(2,1)S(1)} %copy.131), channel_id=1, source_target_pairs={{0,20},{4,24},{8,28},{12,32},{16,36},{20,40},{24,44},{28,48},{32,5... | collective-permute-start | bytes 786440 | tf_op jit(solution)/shard_map/ppermute | solution.py:21
  18.0 47.6 %collective-permute-start.3 = (bf16[2,256,256]{1,2,0:T(8,128)(2,1)S(1)}, bf16[2,256,256]{1,2,0:T(8,128)(2,1)S(1)}, u32[]{:S(2)}, u32[]{:S(2)}) collective-permute-start(bf16[2,256,256]{1,2,0:T(8,128)(2,1)S(1)} %copy.131), channel_id=1, source_target_pairs={{0,16},{4,20},{8,24},{12,28},{16,32},{20,36},{24,40},{28,44},{32,4... | collective-permute-start | bytes 786440 | tf_op jit(solution)/shard_map/ppermute | solution.py:21
  21.6 45.0 %collective-permute-start.2 = (bf16[2,256,256]{1,2,0:T(8,128)(2,1)S(1)}, bf16[2,256,256]{1,2,0:T(8,128)(2,1)S(1)}, u32[]{:S(2)}, u32[]{:S(2)}) collective-permute-start(bf16[2,256,256]{1,2,0:T(8,128)(2,1)S(1)} %copy.131), channel_id=1, source_target_pairs={{0,12},{4,16},{8,20},{12,24},{16,28},{20,32},{24,36},{28,40},{32,4... | collective-permute-start | bytes 786440 | tf_op jit(solution)/shard_map/ppermute | solution.py:21
  26.0 21.6 %all-to-all-start.1 = ((s32[1,64,1]{2,0,1:T(1,128)}), s32[1,64,1]{2,0,1:T(1,128)S(1)}, u32[]{:S(2)}, u32[]{:S(2)}) async-start(s32[1,64,1]{2,0,1:T(1,128)} %copy.163), calls=%async_computation.1 | async-start | bytes 65536 | tf_op jit(solution)/shard_map/all_to_all | solution.py:91
  47.6 48.0 %all-to-all-start = ((bf16[2,64,1,8,256]{4,3,0,2,1:T(8,128)(2,1)}), bf16[2,64,1,8,256]{4,3,0,2,1:T(8,128)(2,1)S(1)}, u32[]{:S(2)}, u32[]{:S(2)}) async-start(bf16[2,64,1,8,256]{4,3,0,2,1:T(8,128)(2,1)} %copy.161), calls=%async_computation | async-start | bytes 1048576 | tf_op jit(solution)/shard_map/all_to_all | solution.py:90
  56.7 19.1 %collective-permute-start.1 = (bf16[2,256,256]{1,2,0:T(8,128)(2,1)S(1)}, bf16[2,256,256]{1,2,0:T(8,128)(2,1)S(1)}, u32[]{:S(2)}, u32[]{:S(2)}) collective-permute-start(bf16[2,256,256]{1,2,0:T(8,128)(2,1)S(1)} %copy.131), channel_id=1, source_target_pairs={{0,8},{4,12},{8,16},{12,20},{16,24},{20,28},{24,32},{28,36},{32,40... | collective-permute-start | bytes 786440 | tf_op jit(solution)/shard_map/ppermute | solution.py:21
  76.8 2.2 %copy-start = (f32[2,256,256,8]{2,1,3,0:T(8,128)S(1)}, f32[2,256,256,8]{2,1,3,0:T(8,128)}, u32[]{:S(2)}) copy-start(f32[2,256,256,8]{2,1,3,0:T(8,128)} %get-tuple-element.55) | copy-start | bytes 12582916
where the time goes:
time: 97.2 us; the launch traced here: 96.7 us
  starting transfers between devices  46.3 us (48%)
  matrix products  17.9 us (18%)
  waiting for transfers between devices  13.1 us (13%)
  other arithmetic  9.38 us (10%)
  local copies, waits for them, and re-layouts  8.91 us (9%)
  between operations  1.02 us (1%)
    ppermute x6, starting transfers between devices, passed_along(): return lax.ppermute(value, axis, pairs)  27.7 us
    all_to_all x1, starting transfers between devices, place_pages(): lax.all_to_all(label, 'seq', split_axis=1, concat_axis=1, tiled=True)  10.7 us
    dot_general x7, matrix products, absorb(): jnp.einsum('kgij,jkd->ikgd', weight.astype(jnp.bfloat16), value_rows, pre...  8.84 us
    dot_general x7, matrix products, absorb(): jnp.einsum('ikgd,jkd->kgij', query_heads, key_rows, preferred_element_typ...  8.42 us
    ppermute x6, waiting for transfers between devices, passed_along(): return lax.ppermute(value, axis, pairs)  8.29 us
    all_to_all x1, starting transfers between devices, place_pages(): lax.all_to_all(outgoing, 'seq', split_axis=1, concat_axis=1, tiled=True)  7.88 us
    reduce_sum x4, other arithmetic, absorb(): total = total * fade + jnp.sum(weight, -1)  7.29 us
    unnamed x8, local copies, waits for them, and re-layouts  5.91 us
  transfers between devices with their start and end apart: 8, of which 2 were waited for; matrix products, arithmetic and copies ran while one was open for 34% of the time, Pallas kernels for 0%

commit v1 on v0

v1 whole, which is shorter than its diff:
```python
import functools
import math

import jax
import jax.numpy as jnp
from jax import lax
from jax.experimental import pallas as pl
from jax.experimental.pallas import tpu as pltpu
from jax.sharding import PartitionSpec as P

MESH = pl.DeviceIdType.MESH
HEAD = 128
GROUP = 8
NX, NH, NZ = 4, 2, 8
NP = NX * NH
PAGES = 32
PAGE = 8
F32 = jnp.float32
BF16 = jnp.bfloat16
LOW = -1e30

A, B, C, D, E, F, G, O3, O2 = range(9)


def kernel(
    slot_ref, q_hbm, kv_hbm, o_ref, pool_ref,
    q_buf, own, kvb, acc, top, pick, sbuf, zbuf, pbuf, row, tab1, tab2, place,
    q_sem, own_sem, loc_sem, kv_recv, kv_send,
    z_recv, z_send, zt_recv, zt_send, p_recv, p_send, pt_recv, pt_send,
):
    s = lax.axis_index("seq")
    tp = lax.axis_index("tp")
    z, p = s // NP, s % NP
    h, x = p // NX, p % NX
    n_seq = NP * NZ
    right = s - x + lax.rem(x + 1, NX)
    left = s - x + lax.rem(x + NX - 1, NX)
    row_up = lax.rem(s + NX, n_seq)
    z_up = lax.rem(s + NP, n_seq)

    own_copy = pltpu.make_async_copy(kv_hbm, own, own_sem)
    own_copy.start()
    heads = q_buf.shape[0]
    q_copies = [
        pltpu.make_async_copy(q_hbm.at[:, pl.ds(i * HEAD, HEAD)], q_buf.at[i], q_sem.at[i])
        for i in range(heads)
    ]
    for copy in q_copies:
        copy.start()

    barrier = pltpu.get_barrier_semaphore()

    def greet(device):
        pl.semaphore_signal(barrier, inc=1, device_id=(device, tp), device_id_type=MESH)

    z_peers = [lax.rem(z + k, NZ) for k in range(1, NZ)]
    p_peers = [lax.rem(p + k, NP) for k in range(1, NP)]
    for peer in z_peers:
        greet(peer * NP + p)
    for peer in p_peers:
        greet(z * NP + peer)
    greet(lax.rem(jnp.where(h == 0, s - NX, s + NX) + n_seq, n_seq))

    lane = lax.broadcasted_iota(jnp.int32, (PAGE, n_seq * PAGE), 1)
    sub = lax.broadcasted_iota(jnp.int32, (PAGE, n_seq * PAGE), 0)
    same_token = (lane % PAGE) == sub
    lane_owner = lane // PAGE
    narrow = lax.broadcasted_iota(jnp.int32, (1, 128), 1)
    slots = jnp.full((1, 128), -1, jnp.int32)
    for j in range(PAGES):
        slot = slot_ref[j]
        pick[j * PAGE : (j + 1) * PAGE, :] = jnp.where(
            jnp.logical_and(same_token, lane_owner == slot // PAGES), 1.0, 0.0
        ).astype(BF16)
        slots = jnp.where(narrow == j, slot, slots)
    row[...] = slots
    own_copy.wait()
    for c in range(2):
        outgoing = lax.dot_general(
            pick[...], own[c], (((0,), (0,)), ((), ())), preferred_element_type=F32
        )
        sbuf[:, :, c * PAGE : (c + 1) * PAGE, :] = outgoing.astype(BF16).reshape(NZ, NP, PAGE, -1)

    pl.semaphore_wait(barrier, NZ - 1 + NP - 1 + 1)

    def hop(src, slot, c, device, number):
        return pltpu.make_async_remote_copy(
            src_ref=src.at[c], dst_ref=kvb.at[slot, c],
            send_sem=kv_send.at[number, c], recv_sem=kv_recv.at[slot, c],
            device_id=(device, tp), device_id_type=MESH,
        )

    def arrived(slot, c):
        hop(kvb.at[slot], slot, c, right, 0).wait_recv()

    last = x == NX - 1
    first = x == 0
    rows_up = [hop(own, C, c, row_up, 0) for c in range(2)]
    old3 = [hop(own, O3, c, z_up, 1) for c in range(2)]
    step1 = [hop(own, A, c, right, 2) for c in range(2)]
    step1_old = [hop(kvb.at[O3], A, c, right, 2) for c in range(2)]
    extra = [hop(own, G, c, left, 3) for c in range(2)]
    old2 = [hop(kvb.at[A], O2, c, z_up, 4) for c in range(2)]
    step2 = [hop(kvb.at[A], B, c, right, 5) for c in range(2)]
    step2_old = [hop(kvb.at[O2], B, c, right, 5) for c in range(2)]
    to_right = [hop(kvb.at[C], D, c, right, 6) for c in range(2)]
    to_left = [hop(kvb.at[C], E, c, left, 7) for c in range(2)]
    to_left2 = [hop(kvb.at[E], F, c, left, 8) for c in range(2)]

    for c in range(2):
        rows_up[c].start()
        pl.when(last)(old3[c].start)
        pl.when(jnp.logical_not(last))(step1[c].start)
        pl.when(first)(extra[c].start)

    stage1 = []
    for k, peer in enumerate(z_peers):
        device = (peer * NP + p, tp)
        stage1.append(pltpu.make_async_remote_copy(
            src_ref=sbuf.at[peer], dst_ref=zbuf.at[:, z], send_sem=z_send.at[k], recv_sem=z_recv.at[z],
            device_id=device, device_id_type=MESH))
        stage1.append(pltpu.make_async_remote_copy(
            src_ref=row, dst_ref=tab1.at[z], send_sem=zt_send.at[k], recv_sem=zt_recv.at[z],
            device_id=device, device_id_type=MESH))
    for copy in stage1:
        copy.start()
    loc1 = pltpu.make_async_copy(sbuf.at[z], zbuf.at[:, z], loc_sem.at[0])
    loc2 = pltpu.make_async_copy(row, tab1.at[z], loc_sem.at[1])
    loc1.start()
    loc2.start()
    for copy in q_copies:
        copy.wait()

    to_exp2 = math.log2(math.e) / math.sqrt(HEAD)
    ones = jnp.ones((own.shape[1], HEAD), BF16)
    tokens = own.shape[1]
    heads_kv = heads // GROUP

    def absorb(block, initial):
        for g in range(heads_kv):
            keys = block[0, :, g * HEAD : (g + 1) * HEAD]
            values = jnp.concatenate([block[1, :, g * HEAD : (g + 1) * HEAD], ones], axis=1)

            def one(i, _):
                head = g * GROUP + i
                score = lax.dot_general(
                    q_buf[head], keys, (((1,), (1,)), ((), ())), preferred_element_type=F32
                ) * to_exp2
                if initial:
                    causal = lax.broadcasted_iota(jnp.int32, (tokens, tokens), 1) <= lax.broadcasted_iota(
                        jnp.int32, (tokens, tokens), 0)
                    score = jnp.where(causal, score, LOW)
                    new_top = jnp.max(score, axis=1, keepdims=True)
                else:
                    new_top = jnp.maximum(top[head][:, :1], jnp.max(score, axis=1, keepdims=True))
                weight = jnp.exp2(score - new_top).astype(BF16)
                mixed = jnp.dot(weight, values, preferred_element_type=F32)
                if initial:
                    acc[head] = mixed
                else:
                    acc[head] = acc[head] * jnp.exp2(top[head][:, :1] - new_top) + mixed
                top[head] = jnp.broadcast_to(new_top, (tokens, HEAD))
                return 0

            lax.fori_loop(0, GROUP, one, 0)

    def absorb_slot(slot, distance):
        pl.when(s >= distance)(lambda: absorb(kvb.at[slot], False))

    absorb(own, True)

    @pl.when(last)
    def _():
        for c in range(2):
            arrived(O3, c)
            step1_old[c].start()

    @pl.when(jnp.logical_not(first))
    def _():
        for c in range(2):
            arrived(A, c)
            pl.when(last)(old2[c].start)
            pl.when(jnp.logical_not(last))(step2[c].start)

    for c in range(2):
        arrived(C, c)
        to_left[c].start()
        to_right[c].start()

    absorb_slot(C, 4)

    @pl.when(first)
    def _():
        for c in range(2):
            arrived(A, c)
            step2[c].start()

    @pl.when(last)
    def _():
        for c in range(2):
            arrived(O2, c)
            step2_old[c].start()

    for c in range(2):
        arrived(E, c)
        to_left2[c].start()

    absorb_slot(A, jnp.where(first, 5, 1))

    for k, peer in enumerate(z_peers):
        pltpu.make_async_remote_copy(
            src_ref=sbuf.at[peer], dst_ref=zbuf.at[:, peer], send_sem=z_send.at[k], recv_sem=z_recv.at[peer],
            device_id=(right, tp), device_id_type=MESH).wait_recv()
        pltpu.make_async_remote_copy(
            src_ref=row, dst_ref=tab1.at[peer], send_sem=zt_send.at[k], recv_sem=zt_recv.at[peer],
            device_id=(right, tp), device_id_type=MESH).wait_recv()
    loc1.wait()
    loc2.wait()
    stage2 = []
    for k, peer in enumerate(p_peers):
        device = (z * NP + peer, tp)
        stage2.append(pltpu.make_async_remote_copy(
            src_ref=zbuf.at[peer], dst_ref=pbuf.at[p], send_sem=p_send.at[k], recv_sem=p_recv.at[p],
            device_id=device, device_id_type=MESH))
        stage2.append(pltpu.make_async_remote_copy(
            src_ref=tab1, dst_ref=tab2.at[p], send_sem=pt_send.at[k], recv_sem=pt_recv.at[p],
            device_id=device, device_id_type=MESH))
    for copy in stage2:
        copy.start()
    loc3 = pltpu.make_async_copy(zbuf.at[p], pbuf.at[p], loc_sem.at[2])
    loc4 = pltpu.make_async_copy(tab1, tab2.at[p], loc_sem.at[3])
    loc3.start()
    loc4.start()

    @pl.when(last)
    def _():
        for c in range(2):
            arrived(G, c)

    absorb_slot(jnp.where(last, G, E), 3)
    for c in range(2):
        arrived(D, c)
    absorb_slot(D, jnp.where(first, 1, 5))
    for c in range(2):
        arrived(B, c)
    absorb_slot(B, jnp.where(x >= 2, 2, 6))
    for c in range(2):
        arrived(F, c)
    absorb_slot(F, jnp.where(x < 2, 2, 6))

    for k, peer in enumerate(p_peers):
        pltpu.make_async_remote_copy(
            src_ref=zbuf.at[peer], dst_ref=pbuf.at[peer], send_sem=p_send.at[k], recv_sem=p_recv.at[peer],
            device_id=(right, tp), device_id_type=MESH).wait_recv()
        pltpu.make_async_remote_copy(
            src_ref=tab1, dst_ref=tab2.at[peer], send_sem=pt_send.at[k], recv_sem=pt_recv.at[peer],
            device_id=(right, tp), device_id_type=MESH).wait_recv()
    loc3.wait()
    loc4.wait()
    wide = lax.broadcasted_iota(jnp.int32, (PAGE, PAGES * PAGE), 1)
    wide_token = (wide % PAGE) == lax.broadcasted_iota(jnp.int32, (PAGE, PAGES * PAGE), 0)
    wide_slot = wide // PAGE
    for source in range(n_seq):
        named = jnp.broadcast_to(tab2[source // NZ, source % NZ], (PAGE, 128))
        mine = jnp.where(named // PAGES == s, named % PAGES + 1, 0)
        within = jnp.sum(mine, axis=1, keepdims=True) - 1
        place[source * PAGE : (source + 1) * PAGE, :] = jnp.where(
            jnp.logical_and(wide_token, wide_slot == within), 1.0, 0.0
        ).astype(BF16)
    for c in range(2):
        pages = pbuf[:, :, c * PAGE : (c + 1) * PAGE, :].reshape(n_seq * PAGE, -1)
        pool_ref[c] = lax.dot_general(
            place[...], pages, (((0,), (0,)), ((), ())), preferred_element_type=F32
        ).astype(BF16)

    for i in range(heads):
        o_ref[:, i * HEAD : (i + 1) * HEAD] = (acc[i, :, :HEAD] / acc[i, :, HEAD:]).astype(BF16)

    for c in range(2):
        rows_up[c].wait_send()
        step1[c].wait_send()
        step2[c].wait_send()
        to_right[c].wait_send()
        to_left[c].wait_send()
        to_left2[c].wait_send()
        pl.when(last)(old3[c].wait_send)
        pl.when(last)(old2[c].wait_send)
        pl.when(first)(extra[c].wait_send)
    for copy in stage1 + stage2:
        copy.wait_send()


def body(queries, new_key_value, page_slot):
    tokens, features = queries.shape
    width = new_key_value.shape[2]
    heads = features // HEAD
    n_seq = NP * NZ
    kv_block = (2, tokens, width)
    dma = pltpu.SemaphoreType.DMA
    attended, pool = pl.pallas_call(
        kernel,
        name="layer",
        out_shape=(
            jax.ShapeDtypeStruct((tokens, features), BF16),
            jax.ShapeDtypeStruct(kv_block, BF16),
        ),
        in_specs=[
            pl.BlockSpec(memory_space=pltpu.SMEM),
            pl.BlockSpec(memory_space=pl.ANY),
            pl.BlockSpec(memory_space=pl.ANY),
        ],
        out_specs=(
            pl.BlockSpec(memory_space=pltpu.VMEM),
            pl.BlockSpec(memory_space=pltpu.VMEM),
        ),
        scratch_shapes=[
            pltpu.VMEM((heads, tokens, HEAD), BF16),
            pltpu.VMEM(kv_block, BF16),
            pltpu.VMEM((9,) + kv_block, BF16),
            pltpu.VMEM((heads, tokens, 2 * HEAD), F32),
            pltpu.VMEM((heads, tokens, HEAD), F32),
            pltpu.VMEM((PAGES * PAGE, n_seq * PAGE), BF16),
            pltpu.VMEM((NZ, NP, 2 * PAGE, width), BF16),
            pltpu.VMEM((NP, NZ, 2 * PAGE, width), BF16),
            pltpu.VMEM((NP, NZ, 2 * PAGE, width), BF16),
            pltpu.VMEM((1, 128), jnp.int32),
            pltpu.VMEM((NZ, 1, 128), jnp.int32),
            pltpu.VMEM((NP, NZ, 1, 128), jnp.int32),
            pltpu.VMEM((n_seq * PAGE, PAGES * PAGE), BF16),
            dma((heads,)), dma, dma((4,)), dma((9, 2)), dma((9, 2)),
            dma((NZ,)), dma((NZ,)), dma((NZ,)), dma((NZ,)),
            dma((NP,)), dma((NP,)), dma((NP,)), dma((NP,)),
        ],
        compiler_params=pltpu.CompilerParams(
            collective_id=0, has_side_effects=True, vmem_limit_bytes=48 << 20
        ),
    )(page_slot, queries, new_key_value)
    return attended, pool.reshape(2, PAGES, PAGE, width)


def solution(mesh):
    return jax.shard_map(
        body,
        mesh=mesh,
        in_specs=(P("seq", "tp"), P(None, "seq", "tp"), P("seq")),
        out_specs=(P("seq", "tp"), P(None, "seq", None, "tp")),
        check_vma=False,
    )
```

time: 97.2 us -> 88.3 us (0.908)
  the two profiles are of different devices: /device:TPU:32 before, /device:TPU:30 now
where the time goes in v1:
time: 88.3 us; the launch traced here: 88.1 us
  Pallas kernels  83 us (94%)
  local copies, waits for them, and re-layouts  4.5 us (5%)
    pallas_call x1, Pallas kernels, body(): pl.pallas_call(kernel, name='layer', out_shape=(jax.ShapeDtypeStruct((tok...  83 us
    unnamed x8, local copies, waits for them, and re-layouts  4.5 us

profile of v1, /device:TPU:30, one launch (start us, length us, event | category | flops | bytes accessed | tf_op | source)
XLA Modules:
  0.0 88.1 jit_solution(10526991625598907720)
XLA Ops:
  0.6 0.0 copy-start
  0.6 1.2 %copy-done = bf16[256,2048]{1,0:T(8,128)(2,1)S(1)} copy-done((bf16[256,2048]{1,0:T(8,128)(2,1)S(1)}, bf16[256,2048]{1,0:T(8,128)(2,1)}, u32[]{:S(2)}) %copy-start) | copy-done | bytes 1048600
  1.9 0.0 copy-start.1
  1.9 0.9 %copy-done.1 = bf16[2,256,256]{2,1,0:T(8,128)(2,1)S(1)} copy-done((bf16[2,256,256]{2,1,0:T(8,128)(2,1)S(1)}, bf16[2,256,256]{2,1,0:T(8,128)(2,1)}, u32[]{:S(2)}) %copy-start.1) | copy-done | bytes 262168
  2.8 0.0 copy-start.2
  2.8 0.7 copy-done.2
  3.5 83.0 %layer.1 = (bf16[256,2048]{1,0:T(8,128)(2,1)S(1)}, bf16[2,256,256]{2,1,0:T(8,128)(2,1)S(1)}) custom-call(s32[32]{0:T(128)S(1)} %copy-done.2, bf16[256,2048]{1,0:T(8,128)(2,1)S(1)} %copy-done, bf16[2,256,256]{2,1,0:T(8,128)(2,1)S(1)} %copy-done.1), custom_call_target="tpu_custom_call" | custom-call | tf_op jit(solution)/shard_map/layer/pallas_call | solution.py:300
  86.4 1.0 %copy.7 = bf16[256,2048]{1,0:T(8,128)(2,1)} copy(bf16[256,2048]{1,0:T(8,128)(2,1)S(1)} %get-tuple-element.8) | data formatting | bytes 2097152
  87.4 0.7 copy.8
Async XLA Ops:
  0.6 1.2 %copy-start = (bf16[256,2048]{1,0:T(8,128)(2,1)S(1)}, bf16[256,2048]{1,0:T(8,128)(2,1)}, u32[]{:S(2)}) copy-start(bf16[256,2048]{1,0:T(8,128)(2,1)} %q_hbm.1) | copy-start | bytes 3145732
  1.9 0.9 %copy-start.1 = (bf16[2,256,256]{2,1,0:T(8,128)(2,1)S(1)}, bf16[2,256,256]{2,1,0:T(8,128)(2,1)}, u32[]{:S(2)}) copy-start(bf16[2,256,256]{2,1,0:T(8,128)(2,1)} %kv_hbm.1) | copy-start | bytes 786436
  2.8 0.7 copy-start.2

commit v2 on v1

v2 whole, which is shorter than its diff:
```python
import functools
import math

import jax
import jax.numpy as jnp
from jax import lax
from jax.experimental import pallas as pl
from jax.experimental.pallas import tpu as pltpu
from jax.sharding import PartitionSpec as P

MESH = pl.DeviceIdType.MESH
HEAD = 128
GROUP = 8
NX, NH, NZ = 4, 2, 8
NP = NX * NH
PAGES = 32
PAGE = 8
F32 = jnp.float32
BF16 = jnp.bfloat16
LOW = -1e30

A, B, C, D, E, F, G, O, O2 = range(9)


def kernel(
    slot_ref, q_hbm, kv_hbm, o_ref, pool_ref,
    q_buf, own, kvb, acc, top, mix, pick, send_k, send_v, mid_k, mid_v, got_k, got_v, row, tab1, tab2, place,
    q_sem, own_sem, loc_sem, kv_recv, kv_send,
    k1_recv, k1_send, v1_recv, v1_send, k2_recv, k2_send, v2_recv, v2_send,
    t1_recv, t1_send, t2_recv, t2_send,
):
    s = lax.axis_index("seq")
    tp = lax.axis_index("tp")
    z, p = s // NP, s % NP
    h, x = p // NX, p % NX
    n_seq = NP * NZ
    right = s - x + lax.rem(x + 1, NX)
    left = s - x + lax.rem(x + NX - 1, NX)
    row_up = lax.rem(s + NX, n_seq)
    z_up = lax.rem(s + NP, n_seq)

    own_copy = pltpu.make_async_copy(kv_hbm, own, own_sem)
    own_copy.start()
    heads = q_buf.shape[0]
    q_copies = [
        pltpu.make_async_copy(q_hbm.at[:, pl.ds(i * HEAD, HEAD)], q_buf.at[i], q_sem.at[i])
        for i in range(heads)
    ]
    for copy in q_copies:
        copy.start()

    barrier = pltpu.get_barrier_semaphore()

    def greet(device):
        pl.semaphore_signal(barrier, inc=1, device_id=(device, tp), device_id_type=MESH)

    z_peers = [lax.rem(z + k, NZ) for k in range(1, NZ)]
    p_peers = [lax.rem(p + k, NP) for k in range(1, NP)]
    for peer in z_peers:
        greet(peer * NP + p)
    for peer in p_peers:
        greet(z * NP + peer)
    greet(lax.rem(jnp.where(h == 0, s - NX, s + NX) + n_seq, n_seq))

    def remote(src, dst, send_sem, recv_sem, device):
        return pltpu.make_async_remote_copy(
            src_ref=src, dst_ref=dst, send_sem=send_sem, recv_sem=recv_sem,
            device_id=(device, tp), device_id_type=MESH,
        )

    half = own.shape[1] // 2
    parts = [(c, pl.ds(i * half, half)) for c in range(2) for i in range(2)]

    def hop(src, slot, device, number):
        return [
            remote(src.at[part], kvb.at[(slot,) + part], kv_send.at[number, k], kv_recv.at[slot, k], device)
            for k, part in enumerate(parts)
        ]

    def arrived(slot, k):
        hop(kvb.at[slot], slot, right, 0)[k].wait_recv()

    first = x == 0
    last = x == NX - 1
    upper = x >= NX // 2
    rows_up = hop(own, C, row_up, 0)
    to_z = hop(kvb.at[O], A, z_up, 1)
    step1 = hop(own, A, right, 2)
    step1_last = hop(own, O, right, 2)
    extra = hop(own, G, left, 3)
    step2 = hop(kvb.at[A], B, right, 4)
    to_z2 = hop(kvb.at[A], O2, z_up, 8)
    step2_old = hop(kvb.at[O2], B, right, 4)
    to_right = hop(kvb.at[C], D, right, 5)
    to_left = hop(kvb.at[C], E, left, 6)
    to_left2 = hop(kvb.at[E], F, left, 7)

    own_copy.wait()
    pl.semaphore_wait(barrier, NZ - 1 + NP - 1 + 1)
    for k in range(4):
        rows_up[k].start()
        pl.when(last)(step1_last[k].start)
        pl.when(jnp.logical_not(last))(step1[k].start)
        pl.when(first)(extra[k].start)

    lane = lax.broadcasted_iota(jnp.int32, (PAGE, n_seq * PAGE), 1)
    sub = lax.broadcasted_iota(jnp.int32, (PAGE, n_seq * PAGE), 0)
    same_token = (lane % PAGE) == sub
    lane_owner = lane // PAGE
    narrow = lax.broadcasted_iota(jnp.int32, (1, 128), 1)
    slots = jnp.full((1, 128), -1, jnp.int32)
    for j in range(PAGES):
        slot = slot_ref[j]
        pick[j * PAGE : (j + 1) * PAGE, :] = jnp.where(
            jnp.logical_and(same_token, lane_owner == slot // PAGES), 1.0, 0.0
        ).astype(BF16)
        slots = jnp.where(narrow == j, slot, slots)
    row[...] = slots
    for c, outgoing in ((0, send_k), (1, send_v)):
        outgoing[...] = lax.dot_general(
            pick[...], own[c], (((0,), (0,)), ((), ())), preferred_element_type=F32
        ).astype(BF16).reshape(NZ, NP, PAGE, -1)

    stage2 = []

    def start_values():
        for copy in stage1_v:
            copy.start()

    def pass_values():
        for k, peer in enumerate(p_peers):
            remote(send_v.at[:, peer], mid_v.at[:, peer], v1_send.at[k], v1_recv.at[peer], right).wait_recv()
        local1[2].wait()
        local2[0].start()
        for k, peer in enumerate(z_peers):
            stage2.append(remote(mid_v.at[peer], got_v.at[:, z], v2_send.at[k], v2_recv.at[z], peer * NP + p))
            stage2[-1].start()

    def pass_keys():
        for k, peer in enumerate(z_peers):
            remote(send_k.at[peer], mid_k.at[:, peer], k1_send.at[k], k1_recv.at[peer], right).wait_recv()
            remote(row, tab1.at[peer], t1_send.at[k], t1_recv.at[peer], right).wait_recv()
        local1[0].wait()
        local1[1].wait()
        local2[1].start()
        local2[2].start()
        for k, peer in enumerate(p_peers):
            stage2.append(remote(mid_k.at[peer], got_k.at[p], k2_send.at[k], k2_recv.at[p], z * NP + peer))
            stage2[-1].start()
            stage2.append(remote(tab1, tab2.at[p], t2_send.at[k], t2_recv.at[p], z * NP + peer))
            stage2[-1].start()

    local2 = [
        pltpu.make_async_copy(mid_v.at[z], got_v.at[:, z], loc_sem.at[3]),
        pltpu.make_async_copy(mid_k.at[p], got_k.at[p], loc_sem.at[4]),
        pltpu.make_async_copy(tab1, tab2.at[p], loc_sem.at[5]),
    ]
    stage1 = []
    for k, peer in enumerate(z_peers):
        stage1.append(remote(send_k.at[peer], mid_k.at[:, z], k1_send.at[k], k1_recv.at[z], peer * NP + p))
        stage1.append(remote(row, tab1.at[z], t1_send.at[k], t1_recv.at[z], peer * NP + p))
    stage1_v = [
        remote(send_v.at[:, peer], mid_v.at[:, p], v1_send.at[k], v1_recv.at[p], z * NP + peer)
        for k, peer in enumerate(p_peers)
    ]
    local1 = [
        pltpu.make_async_copy(send_k.at[z], mid_k.at[:, z], loc_sem.at[0]),
        pltpu.make_async_copy(row, tab1.at[z], loc_sem.at[1]),
        pltpu.make_async_copy(send_v.at[:, p], mid_v.at[:, p], loc_sem.at[2]),
    ]
    for copy in stage1 + local1:
        copy.start()
    start_values()
    for copy in q_copies:
        copy.wait()

    to_exp2 = math.log2(math.e) / math.sqrt(HEAD)
    tokens = own.shape[1]
    heads_kv = heads // GROUP

    def absorb(block, initial):
        for g in range(heads_kv):
            mix[g, :, :HEAD] = block[1, :, g * HEAD : (g + 1) * HEAD]

            def one(i, _):
                head = g * GROUP + i
                score = lax.dot_general(
                    q_buf[head], block[0, :, g * HEAD : (g + 1) * HEAD],
                    (((1,), (1,)), ((), ())), preferred_element_type=F32,
                ) * to_exp2
                if initial:
                    causal = lax.broadcasted_iota(jnp.int32, (tokens, tokens), 1) <= lax.broadcasted_iota(
                        jnp.int32, (tokens, tokens), 0)
                    score = jnp.where(causal, score, LOW)
                    new_top = jnp.broadcast_to(jnp.max(score, axis=1, keepdims=True), (tokens, HEAD))
                else:
                    old_top = top[head]
                    new_top = jnp.maximum(old_top, jnp.max(score, axis=1, keepdims=True))
                weight = jnp.exp2(score - jnp.concatenate([new_top, new_top], axis=1)).astype(BF16)
                mixed = jnp.dot(weight, mix[g], preferred_element_type=F32)
                top[head] = new_top
                if initial:
                    acc[head] = mixed
                else:
                    fade = jnp.exp2(old_top - new_top)
                    acc[head] = acc[head] * jnp.concatenate([fade, fade], axis=1) + mixed
                return 0

            lax.fori_loop(0, GROUP, one, 0, unroll=True)

    def absorb_slot(slot, distance):
        pl.when(s >= distance)(lambda: absorb(kvb.at[slot], False))

    mix[:, :, HEAD:] = jnp.ones((heads_kv, tokens, HEAD), BF16)
    absorb(own, True)

    def from_row(k):
        arrived(C, k)
        to_left[k].start()
        to_right[k].start()

    for k in range(4):
        @pl.when(first)
        def _():
            arrived(O, k)
            to_z[k].start()

        @pl.when(jnp.logical_not(first))
        def _():
            arrived(A, k)
            pl.when(last)(to_z2[k].start)
            pl.when(jnp.logical_not(last))(step2[k].start)

        if k >= 1:
            from_row(k - 1)
    from_row(3)

    pass_values()
    pass_keys()
    absorb_slot(C, 4)

    for k in range(4):
        @pl.when(first)
        def _():
            arrived(A, k)
            step2[k].start()

        @pl.when(last)
        def _():
            arrived(O2, k)
            step2_old[k].start()

        arrived(E, k)
        to_left2[k].start()

    absorb_slot(A, jnp.where(first, 5, 1))

    @pl.when(last)
    def _():
        for k in range(4):
            arrived(G, k)

    absorb_slot(jnp.where(last, G, E), 3)
    for slot, distance in (
        (B, jnp.where(upper, 2, 6)),
        (D, jnp.where(first, 1, 5)),
        (F, jnp.where(upper, 6, 2)),
    ):
        for k in range(4):
            arrived(slot, k)
        absorb_slot(slot, distance)

    for i in range(heads):
        o_ref[:, i * HEAD : (i + 1) * HEAD] = (acc[i, :, :HEAD] / acc[i, :, HEAD:]).astype(BF16)

    for k, peer in enumerate(z_peers):
        remote(mid_v.at[peer], got_v.at[:, peer], v2_send.at[k], v2_recv.at[peer], right).wait_recv()
    for k, peer in enumerate(p_peers):
        remote(mid_k.at[peer], got_k.at[peer], k2_send.at[k], k2_recv.at[peer], right).wait_recv()
        remote(tab1, tab2.at[peer], t2_send.at[k], t2_recv.at[peer], right).wait_recv()
    for copy in local2:
        copy.wait()
    wide = lax.broadcasted_iota(jnp.int32, (PAGE, PAGES * PAGE), 1)
    wide_token = (wide % PAGE) == lax.broadcasted_iota(jnp.int32, (PAGE, PAGES * PAGE), 0)
    wide_slot = wide // PAGE
    for source in range(n_seq):
        named = jnp.broadcast_to(tab2[source // NZ, source % NZ], (PAGE, 128))
        mine = jnp.where(named // PAGES == s, named % PAGES + 1, 0)
        within = jnp.sum(mine, axis=1, keepdims=True) - 1
        place[source * PAGE : (source + 1) * PAGE, :] = jnp.where(
            jnp.logical_and(wide_token, wide_slot == within), 1.0, 0.0
        ).astype(BF16)
    for c, pages in ((0, got_k), (1, got_v)):
        pool_ref[c] = lax.dot_general(
            place[...], pages[...].reshape(n_seq * PAGE, -1), (((0,), (0,)), ((), ())), preferred_element_type=F32
        ).astype(BF16)

    for k in range(4):
        rows_up[k].wait_send()
        pl.when(first)(to_z[k].wait_send)
        pl.when(last)(to_z2[k].wait_send)
        step1[k].wait_send()
        pl.when(first)(extra[k].wait_send)
        step2[k].wait_send()
        to_right[k].wait_send()
        to_left[k].wait_send()
        to_left2[k].wait_send()
    for copy in stage1 + stage1_v + stage2:
        copy.wait_send()


def body(queries, new_key_value, page_slot):
    tokens, features = queries.shape
    width = new_key_value.shape[2]
    heads = features // HEAD
    n_seq = NP * NZ
    kv_block = (2, tokens, width)
    dma = pltpu.SemaphoreType.DMA
    attended, pool = pl.pallas_call(
        kernel,
        name="layer",
        out_shape=(
            jax.ShapeDtypeStruct((tokens, features), BF16),
            jax.ShapeDtypeStruct(kv_block, BF16),
        ),
        in_specs=[
            pl.BlockSpec(memory_space=pltpu.SMEM),
            pl.BlockSpec(memory_space=pl.ANY),
            pl.BlockSpec(memory_space=pl.ANY),
        ],
        out_specs=(
            pl.BlockSpec(memory_space=pltpu.VMEM),
            pl.BlockSpec(memory_space=pltpu.VMEM),
        ),
        scratch_shapes=[
            pltpu.VMEM((heads, tokens, HEAD), BF16),
            pltpu.VMEM(kv_block, BF16),
            pltpu.VMEM((9,) + kv_block, BF16),
            pltpu.VMEM((heads, tokens, 2 * HEAD), F32),
            pltpu.VMEM((heads, tokens, HEAD), F32),
            pltpu.VMEM((width // HEAD, tokens, 2 * HEAD), BF16),
            pltpu.VMEM((PAGES * PAGE, n_seq * PAGE), BF16),
            *[pltpu.VMEM((NP, NP, PAGE, width), BF16)] * 6,
            pltpu.VMEM((1, 128), jnp.int32),
            pltpu.VMEM((NZ, 1, 128), jnp.int32),
            pltpu.VMEM((NP, NZ, 1, 128), jnp.int32),
            pltpu.VMEM((n_seq * PAGE, PAGES * PAGE), BF16),
            dma((heads,)), dma, dma((6,)), dma((9, 4)), dma((9, 4)),
            *[dma((NP,))] * 12,
        ],
        compiler_params=pltpu.CompilerParams(
            collective_id=0, has_side_effects=True, vmem_limit_bytes=60 * 1024 * 1024
        ),
    )(page_slot, queries, new_key_value)
    return attended, pool.reshape(2, PAGES, PAGE, width)


def solution(mesh):
    return jax.shard_map(
        body,
        mesh=mesh,
        in_specs=(P("seq", "tp"), P(None, "seq", "tp"), P("seq")),
        out_specs=(P("seq", "tp"), P(None, "seq", None, "tp")),
        check_vma=False,
    )
```

time: 88.3 us -> 47.2 us (0.53)
  the two profiles are of different devices: /device:TPU:30 before, /device:TPU:48 now
where the time goes in v2:
time: 47.2 us; the launch traced here: 47 us
  Pallas kernels  43.3 us (92%)
  local copies, waits for them, and re-layouts  3.05 us (6%)
  between operations  0.65 us (1%)
    pallas_call x1, Pallas kernels, body(): pl.pallas_call(kernel, name='layer', out_shape=(jax.ShapeDtypeStruct((tok...  43.3 us
    unnamed x4, local copies, waits for them, and re-layouts  3.05 us

profile of v2, /device:TPU:48, one launch (start us, length us, event | category | flops | bytes accessed | tf_op | source)
XLA Modules:
  0.0 47.0 jit_solution(3863167001279005639)
XLA Ops:
  0.6 43.3 %layer.1 = (bf16[256,2048]{1,0:T(8,128)(2,1)}, bf16[2,256,256]{2,1,0:T(8,128)(2,1)}) custom-call(s32[32]{0:T(128)} %slot_ref.1, bf16[256,2048]{1,0:T(8,128)(2,1)} %q_hbm.1, bf16[2,256,256]{2,1,0:T(8,128)(2,1)} %kv_hbm.1), custom_call_target="tpu_custom_call" | custom-call | tf_op jit(solution)/shard_map/layer/pallas_call | solution.py:319
  44.0 0.0 copy-start
  44.0 2.3 %copy.7 = bf16[256,2048]{1,0:T(8,128)(2,1)} copy(bf16[256,2048]{1,0:T(8,128)(2,1)} %get-tuple-element.8) | data formatting | bytes 2097152
  46.3 0.0 copy-done
  46.3 0.7 %copy.8 = bf16[2,32,8,256]{3,2,1,0:T(8,128)(2,1)} copy(bf16[2,32,8,256]{3,2,1,0:T(8,128)(2,1)S(1)} %bitcast.1) | data formatting | bytes 524288
Async XLA Ops:
  44.0 2.4 %copy-start = (bf16[2,256,256]{2,1,0:T(8,128)(2,1)S(1)}, bf16[2,256,256]{2,1,0:T(8,128)(2,1)}, u32[]{:S(2)}) copy-start(bf16[2,256,256]{2,1,0:T(8,128)(2,1)} %get-tuple-element.5) | copy-start | bytes 786436

commit v3 on v2

--- a/solution.py
+++ b/solution.py
@@ -95,14 +95,6 @@
     to_left = hop(kvb.at[C], E, left, 6)
     to_left2 = hop(kvb.at[E], F, left, 7)
 
-    own_copy.wait()
-    pl.semaphore_wait(barrier, NZ - 1 + NP - 1 + 1)
-    for k in range(4):
-        rows_up[k].start()
-        pl.when(last)(step1_last[k].start)
-        pl.when(jnp.logical_not(last))(step1[k].start)
-        pl.when(first)(extra[k].start)
-
     lane = lax.broadcasted_iota(jnp.int32, (PAGE, n_seq * PAGE), 1)
     sub = lax.broadcasted_iota(jnp.int32, (PAGE, n_seq * PAGE), 0)
     same_token = (lane % PAGE) == sub
@@ -116,6 +108,14 @@
         ).astype(BF16)
         slots = jnp.where(narrow == j, slot, slots)
     row[...] = slots
+    own_copy.wait()
+    pl.semaphore_wait(barrier, NZ - 1 + NP - 1 + 1)
+    for k in range(4):
+        rows_up[k].start()
+        pl.when(last)(step1_last[k].start)
+        pl.when(jnp.logical_not(last))(step1[k].start)
+        pl.when(first)(extra[k].start)
+
     for c, outgoing in ((0, send_k), (1, send_v)):
         outgoing[...] = lax.dot_general(
             pick[...], own[c], (((0,), (0,)), ((), ())), preferred_element_type=F32
@@ -171,8 +171,6 @@
     for copy in stage1 + local1:
         copy.start()
     start_values()
-    for copy in q_copies:
-        copy.wait()
 
     to_exp2 = math.log2(math.e) / math.sqrt(HEAD)
     tokens = own.shape[1]
@@ -211,8 +209,6 @@
     def absorb_slot(slot, distance):
         pl.when(s >= distance)(lambda: absorb(kvb.at[slot], False))
 
-    mix[:, :, HEAD:] = jnp.ones((heads_kv, tokens, HEAD), BF16)
-    absorb(own, True)
 
     def from_row(k):
         arrived(C, k)
@@ -235,10 +231,10 @@
             from_row(k - 1)
     from_row(3)
 
-    pass_values()
-    pass_keys()
-    absorb_slot(C, 4)
-
+    for copy in q_copies:
+        copy.wait()
+    mix[:, :, HEAD:] = jnp.ones((heads_kv, tokens, HEAD), BF16)
+    absorb(own, True)
     for k in range(4):
         @pl.when(first)
         def _():
@@ -250,6 +246,11 @@
             arrived(O2, k)
             step2_old[k].start()
 
+    pass_values()
+    absorb_slot(C, 4)
+    pass_keys()
+
+    for k in range(4):
         arrived(E, k)
         to_left2[k].start()
 

time: 47.2 us -> 47.7 us (1.011)
  the two profiles are of different devices: /device:TPU:48 before, /device:TPU:30 now
where the time goes in v3:
time: 47.7 us; the launch traced here: 47.1 us
  Pallas kernels  43.4 us (91%)
  local copies, waits for them, and re-layouts  3.05 us (6%)
  between operations  0.65 us (1%)
    pallas_call x1, Pallas kernels, body(): pl.pallas_call(kernel, name='layer', out_shape=(jax.ShapeDtypeStruct((tok...  43.4 us
    unnamed x4, local copies, waits for them, and re-layouts  3.05 us

profile of v3, /device:TPU:30, one launch (start us, length us, event | category | flops | bytes accessed | tf_op | source)
XLA Modules:
  0.0 47.1 jit_solution(3749627659356487)
XLA Ops:
  0.6 43.4 %layer.1 = (bf16[256,2048]{1,0:T(8,128)(2,1)}, bf16[2,256,256]{2,1,0:T(8,128)(2,1)}) custom-call(s32[32]{0:T(128)} %slot_ref.1, bf16[256,2048]{1,0:T(8,128)(2,1)} %q_hbm.1, bf16[2,256,256]{2,1,0:T(8,128)(2,1)} %kv_hbm.1), custom_call_target="tpu_custom_call" | custom-call | tf_op jit(solution)/shard_map/layer/pallas_call | solution.py:320
  44.1 0.0 copy-start
  44.1 2.3 %copy.7 = bf16[256,2048]{1,0:T(8,128)(2,1)} copy(bf16[256,2048]{1,0:T(8,128)(2,1)} %get-tuple-element.8) | data formatting | bytes 2097152
  46.4 0.0 copy-done
  46.4 0.7 %copy.8 = bf16[2,32,8,256]{3,2,1,0:T(8,128)(2,1)} copy(bf16[2,32,8,256]{3,2,1,0:T(8,128)(2,1)S(1)} %bitcast.1) | data formatting | bytes 524288
Async XLA Ops:
  44.1 2.4 %copy-start = (bf16[2,256,256]{2,1,0:T(8,128)(2,1)S(1)}, bf16[2,256,256]{2,1,0:T(8,128)(2,1)}, u32[]{:S(2)}) copy-start(bf16[2,256,256]{2,1,0:T(8,128)(2,1)} %get-tuple-element.5) | copy-start | bytes 786436
